TPU v7x, 512 devices: a whole 4x4x16 slice. The times are simulated.
512 devices in a mesh: vec: 64 (over y, z), row: 8 (over x, core).
Axes of the slice: x: 4, y: 4, z: 16, core: 2. Of those that a mesh axis runs over, the one named last changes fastest.
Arguments:
- vectors: bfloat16 [8, 4096, 1024], P('row', 'vec'), may hold values from -6 to 6
- rotation: bfloat16 [1024, 1024], P(None, 'vec'), may hold values from -0.1875 to 0.1875
- blocks: bfloat16 [256, 8, 128, 128], P('row'), may hold values from -0.125 to 0.125
- column_blocks: int32 [256, 8], P('row'), may hold values from -2 to 257, as said below
Outputs:
- filtered: bfloat16 [8, 4096, 1024], P('row', 'vec')
Inputs may be any that keep to these rules, and one draw needn't show every extreme that they name: `column_blocks`: block row r of partition p = r // 32 lists 8 distinct column blocks between p * 32 - 2 and p * 32 + 33; the first block row of every partition lists the lowest of these and the last one the highest; column blocks outside 0 to 255 stand for zeros.
All inputs are finite; a program needn't handle non-finite values.
Results may differ from a plain program's by a relative error of at most 0.006.
Values may be sent and summed in bfloat16 or wider, within the bound.
A program may use at most 64 MiB of HBM per device.

v0:
```python
import jax
import jax.numpy as jnp
from jax import lax
from jax.sharding import PartitionSpec as P

BS = 128
HB = 2
STEPS = 4
centre = 0.3
half_width = 1.2


def with_halo(block, sides, width):
    for axis, dim in sides:
        count = lax.axis_size(axis)
        forward = [(i, i + 1) for i in range(count - 1)]
        backward = [(target, source) for source, target in forward]
        low = lax.ppermute(
            lax.slice_in_dim(block, block.shape[dim] - width, None, axis=dim), axis, forward
        )
        high = lax.ppermute(lax.slice_in_dim(block, 0, width, axis=dim), axis, backward)
        block = jnp.concatenate([low, block, high], axis=dim)
    return block


def apply_matrix(operand, blocks, offsets):
    extended = with_halo(operand, (("row", 1),), HB * BS)
    stacked = extended.reshape(extended.shape[0], -1, BS)
    picked = stacked[:, offsets]
    product = jnp.einsum("rjab,krjb->kra", blocks, picked, preferred_element_type=jnp.float32)
    return product.reshape(extended.shape[0], -1)


def filter_panel(vec_panel, blocks, offsets):
    previous = vec_panel.astype(jnp.float32)
    current = (apply_matrix(vec_panel, blocks, offsets) - centre * previous) / half_width
    for turn_index in range(STEPS - 1):
        operand = current.astype(jnp.bfloat16)
        following = (
            2.0 * (apply_matrix(operand, blocks, offsets) - centre * current) / half_width
            - previous
        )
        previous = current
        current = following
    return current.astype(jnp.bfloat16)


def local(vectors, rotation, blocks, column_blocks):
    local_rows = vectors[0]
    offsets = column_blocks - (lax.axis_index("row") * column_blocks.shape[0] - HB)
    contract = (((0,), (1,)), ((), ()))
    vec_panel = lax.dot_general(
        rotation,
        lax.all_gather(local_rows, "vec", axis=0, tiled=True),
        contract,
        preferred_element_type=jnp.float32,
    ).astype(jnp.bfloat16)
    filtered = filter_panel(vec_panel, blocks, offsets)
    returned = lax.all_to_all(filtered, "vec", split_axis=1, concat_axis=0, tiled=True)
    return jnp.transpose(returned)[None]


def solution(mesh):
    placed = (P("row", "vec", None), P(None, "vec"), P("row", None, None, None), P("row", None))
    return jax.shard_map(
        local, mesh=mesh, in_specs=placed, out_specs=P("row", "vec", None), check_vma=False
    )
```

profile of v0, /device:TPU:1, one launch (start us, length us, event | category | flops | bytes accessed | tf_op | source)
XLA Modules:
  0.0 266.6 jit_solution(13129486595092253713)
XLA Ops:
  6.5 0.0 copy-start
  6.5 0.0 all-gather.3.cloned.1.call-start
  6.5 0.7 all-gather.3.cloned.1.call-update
  7.3 0.7 compare_select_fusion
  8.0 0.1 copy.14
  8.0 0.1 reshape.37
  8.1 156.6 %all-gather.3.cloned.1.call-done = bf16[1,4096,1024]{2,1,0:T(8,128)(2,1)} async-done(((bf16[1,64,1024]{2,1,0:T(8,128)(2,1)}), bf16[1,4096,1024]{2,1,0:T(8,128)(2,1)}) %all-gather.3.cloned.1.call-update) | async-done | bytes 8388624 | tf_op jit(solution)/shard_map/all_gather | solution.py:54
  164.7 0.0 copy-done
  164.7 5.7 %fusion.2 = bf16[16,4096]{1,0:T(8,128)(2,1)S(1)} fusion(bf16[1024,16]{0,1:T(8,128)(2,1)S(1)} %copy-done, bf16[1,4096,1024]{2,1,0:T(8,128)(2,1)} %all-gather.3.cloned.1.call-done), kind=kOutput, calls=%fused_computation.6 | convolution fusion | flops 134283264 | bytes 8552448 | tf_op jit(solution)/shard_map/dot_general | solution.py:52
  170.4 11.5 %collective-permute-start = (bf16[16,256]{1,0:T(8,128)(2,1)S(1)}, bf16[16,256]{1,0:T(8,128)(2,1)S(1)}, u32[]{:S(2)}, u32[]{:S(2)}) collective-permute-start(bf16[16,256]{1,0:T(8,128)(2,1)S(1)} %get-tuple-element.11), channel_id=1, source_target_pairs={{0,1},{1,2},{2,3},{3,4},{4,5},{5,6},{6,7},{8,9},{9,10},{10,11},{11... | collective-permute-start | bytes 24584 | tf_op jit(solution)/shard_map/ppermute | solution.py:18
  181.8 1.9 collective-permute-start.1
  183.8 0.0 collective-permute-done
  183.8 3.0 %collective-permute-done.1 = bf16[16,256]{1,0:T(8,128)(2,1)S(1)} collective-permute-done((bf16[16,256]{1,0:T(8,128)(2,1)S(1)}, bf16[16,256]{1,0:T(8,128)(2,1)S(1)}, u32[]{:S(2)}, u32[]{:S(2)}) %collective-permute-start.1) | collective-permute-done | bytes 8224 | tf_op jit(solution)/shard_map/ppermute | solution.py:21
  186.8 0.8 gather_fusion
  187.7 5.7 %convolution_bitcast_fusion.3 = f32[32,2,8,128]{3,2,1,0:T(8,128)S(1)} fusion(bf16[16,32,8,128]{3,0,2,1:T(8,128)(2,1)S(1)} %bitcast.130, bf16[32,8,128,128]{3,2,1,0:T(8,128)(2,1)} %param.6), kind=kOutput, calls=%fused_computation.10 | convolution fusion | flops 134217728 | bytes 9699328 | tf_op jit(solution)/shard_map/rjab,krjb->kra/dot_general | solution.py:30
  193.4 0.1 multiply_convert_fusion
  193.4 1.9 collective-permute-start.2
  195.4 2.4 collective-permute-start.3
  197.8 0.0 collective-permute-done.2
  197.8 2.6 collective-permute-done.3
  200.4 0.8 gather_fusion.1
  201.2 5.7 %convolution_bitcast_fusion.2 = f32[32,2,8,128]{3,2,1,0:T(8,128)S(1)} fusion(bf16[16,32,8,128]{3,0,2,1:T(8,128)(2,1)S(1)} %bitcast.131, bf16[32,8,128,128]{3,2,1,0:T(8,128)(2,1)} %param.6), kind=kOutput, calls=%fused_computation.9 | convolution fusion | flops 134217728 | bytes 9699328 | tf_op jit(solution)/shard_map/rjab,krjb->kra/dot_general | solution.py:30
  206.9 0.1 fusion.13
  207.0 1.9 collective-permute-start.4
  209.0 2.4 collective-permute-start.5
  211.3 0.0 collective-permute-done.4
  211.4 2.6 collective-permute-done.5
  214.0 0.8 gather_fusion.2
  214.8 5.7 %convolution_bitcast_fusion.1 = f32[32,2,8,128]{3,2,1,0:T(8,128)S(1)} fusion(bf16[16,32,8,128]{3,0,2,1:T(8,128)(2,1)S(1)} %bitcast.132, bf16[32,8,128,128]{3,2,1,0:T(8,128)(2,1)} %param.6), kind=kOutput, calls=%fused_computation.8 | convolution fusion | flops 134217728 | bytes 9699328 | tf_op jit(solution)/shard_map/rjab,krjb->kra/dot_general | solution.py:30
  220.5 0.1 fusion.12
  220.6 1.9 collective-permute-start.6
  222.6 2.4 collective-permute-start.7
  225.0 0.0 collective-permute-done.6
  225.0 2.6 collective-permute-done.7
  227.6 0.8 gather_fusion.3
  228.4 5.7 %convolution_bitcast_fusion = f32[32,2,8,128]{3,2,1,0:T(8,128)S(1)} fusion(bf16[16,32,8,128]{3,0,2,1:T(8,128)(2,1)S(1)} %bitcast.129, bf16[32,8,128,128]{3,2,1,0:T(8,128)(2,1)} %param.6), kind=kOutput, calls=%fused_computation.7 | convolution fusion | flops 134217728 | bytes 9699328 | tf_op jit(solution)/shard_map/rjab,krjb->kra/dot_general | solution.py:30
  234.1 0.2 fusion.8
  234.3 0.2 all_to_all.14
  234.5 0.2 copy.72
  234.7 0.2 reshape.80
  234.9 23.9 %all_to_all.19 = bf16[64,2,512]{2,1,0:T(2,128)(2,1)S(1)} all-to-all(bf16[64,2,512]{2,1,0:T(2,128)(2,1)S(1)} %reshape.80), channel_id=1, replica_groups=mesh['vec'=64,'row'=8] {'vec'}, dimensions={0} | all-to-all | bytes 262144 | tf_op jit(solution)/shard_map/all_to_all | solution.py:59
  258.8 0.2 reshape.81
  259.0 0.8 copy.24
  (9 shorter events, 0.1 us)
Async XLA Ops:
  6.5 158.2 %copy-start = (bf16[1024,16]{0,1:T(8,128)(2,1)S(1)}, bf16[1024,16]{0,1:T(8,128)(2,1)}, u32[]{:S(2)}) copy-start(bf16[1024,16]{0,1:T(8,128)(2,1)} %param.5) | copy-start | bytes 98308
  6.5 158.2 %all-gather.3.cloned.1.call-start = ((), (), s32[]{:S(2)}) async-start(), calls=%async_computation.1 | async-start | bytes 8519680 | tf_op jit(solution)/shard_map/all_gather | solution.py:54
  170.4 13.4 %collective-permute-start = (bf16[16,256]{1,0:T(8,128)(2,1)S(1)}, bf16[16,256]{1,0:T(8,128)(2,1)S(1)}, u32[]{:S(2)}, u32[]{:S(2)}) collective-permute-start(bf16[16,256]{1,0:T(8,128)(2,1)S(1)} %get-tuple-element.11), channel_id=1, source_target_pairs={{0,1},{1,2},{2,3},{3,4},{4,5},{5,6},{6,7},{8,9},{9,10},{10,11},{11... | collective-permute-start | bytes 24584 | tf_op jit(solution)/shard_map/ppermute | solution.py:18
  181.8 5.0 %collective-permute-start.1 = (bf16[16,256]{1,0:T(8,128)(2,1)S(1)}, bf16[16,256]{1,0:T(8,128)(2,1)S(1)}, u32[]{:S(2)}, u32[]{:S(2)}) collective-permute-start(bf16[16,256]{1,0:T(8,128)(2,1)S(1)} %get-tuple-element.12), channel_id=1, source_target_pairs={{1,0},{2,1},{3,2},{4,3},{5,4},{6,5},{7,6},{9,8},{10,9},{11,10},{12... | collective-permute-start | bytes 24584 | tf_op jit(solution)/shard_map/ppermute | solution.py:21
  193.4 4.3 %collective-permute-start.2 = (bf16[16,256]{1,0:T(8,128)(2,1)S(1)}, bf16[16,256]{1,0:T(8,128)(2,1)S(1)}, u32[]{:S(2)}, u32[]{:S(2)}) collective-permute-start(bf16[16,256]{1,0:T(8,128)(2,1)S(1)} %get-tuple-element.9), channel_id=1, source_target_pairs={{0,1},{1,2},{2,3},{3,4},{4,5},{5,6},{6,7},{8,9},{9,10},{10,11},{11... | collective-permute-start | bytes 24584 | tf_op jit(solution)/shard_map/ppermute | solution.py:18
  195.4 5.0 %collective-permute-start.3 = (bf16[16,256]{1,0:T(8,128)(2,1)S(1)}, bf16[16,256]{1,0:T(8,128)(2,1)S(1)}, u32[]{:S(2)}, u32[]{:S(2)}) collective-permute-start(bf16[16,256]{1,0:T(8,128)(2,1)S(1)} %get-tuple-element.10), channel_id=1, source_target_pairs={{1,0},{2,1},{3,2},{4,3},{5,4},{6,5},{7,6},{9,8},{10,9},{11,10},{12... | collective-permute-start | bytes 24584 | tf_op jit(solution)/shard_map/ppermute | solution.py:21
  207.0 4.3 %collective-permute-start.4 = (bf16[16,256]{1,0:T(8,128)(2,1)S(1)}, bf16[16,256]{1,0:T(8,128)(2,1)S(1)}, u32[]{:S(2)}, u32[]{:S(2)}) collective-permute-start(bf16[16,256]{1,0:T(8,128)(2,1)S(1)} %get-tuple-element.7), channel_id=1, source_target_pairs={{0,1},{1,2},{2,3},{3,4},{4,5},{5,6},{6,7},{8,9},{9,10},{10,11},{11... | collective-permute-start | bytes 24584 | tf_op jit(solution)/shard_map/ppermute | solution.py:18
  209.0 5.0 %collective-permute-start.5 = (bf16[16,256]{1,0:T(8,128)(2,1)S(1)}, bf16[16,256]{1,0:T(8,128)(2,1)S(1)}, u32[]{:S(2)}, u32[]{:S(2)}) collective-permute-start(bf16[16,256]{1,0:T(8,128)(2,1)S(1)} %get-tuple-element.8), channel_id=1, source_target_pairs={{1,0},{2,1},{3,2},{4,3},{5,4},{6,5},{7,6},{9,8},{10,9},{11,10},{12... | collective-permute-start | bytes 24584 | tf_op jit(solution)/shard_map/ppermute | solution.py:21
  220.6 4.3 %collective-permute-start.6 = (bf16[16,256]{1,0:T(8,128)(2,1)S(1)}, bf16[16,256]{1,0:T(8,128)(2,1)S(1)}, u32[]{:S(2)}, u32[]{:S(2)}) collective-permute-start(bf16[16,256]{1,0:T(8,128)(2,1)S(1)} %get-tuple-element.5), channel_id=1, source_target_pairs={{0,1},{1,2},{2,3},{3,4},{4,5},{5,6},{6,7},{8,9},{9,10},{10,11},{11... | collective-permute-start | bytes 24584 | tf_op jit(solution)/shard_map/ppermute | solution.py:18
  222.6 5.0 %collective-permute-start.7 = (bf16[16,256]{1,0:T(8,128)(2,1)S(1)}, bf16[16,256]{1,0:T(8,128)(2,1)S(1)}, u32[]{:S(2)}, u32[]{:S(2)}) collective-permute-start(bf16[16,256]{1,0:T(8,128)(2,1)S(1)} %get-tuple-element.6), channel_id=1, source_target_pairs={{1,0},{2,1},{3,2},{4,3},{5,4},{6,5},{7,6},{9,8},{10,9},{11,10},{12... | collective-permute-start | bytes 24584 | tf_op jit(solution)/shard_map/ppermute | solution.py:21
Sparse Core Ops, SparseCore 0:
  10.3 154.3 all-gather.2
where the time goes:
time: 267 us
  waiting for transfers between devices  168 us (63%)
  matrix products  28.3 us (11%)
  starting transfers between devices  26.3 us (10%)
  blocking collectives  23.9 us (9%)
  between operations  13.6 us (5%)
  local copies, waits for them, and re-layouts  5.19 us (2%)
    all_gather x1, waiting for transfers between devices, local(): lax.all_gather(local_rows, 'vec', axis=0, tiled=True)  157 us
    all_to_all x1, blocking collectives, local(): lax.all_to_all(filtered, 'vec', split_axis=1, concat_axis=0, tiled=True)  23.9 us
    dot_general x4, matrix products, apply_matrix(): jnp.einsum('rjab,krjb->kra', blocks, picked, preferred_element_type=jnp.f...  22.6 us
    ppermute x4, starting transfers between devices, with_halo(): lax.ppermute(lax.slice_in_dim(block, block.shape[dim] - width, None, axis...  17.3 us
    ppermute x4, waiting for transfers between devices, with_halo(): lax.ppermute(lax.slice_in_dim(block, 0, width, axis=dim), axis, backward)  10.7 us
    ppermute x4, starting transfers between devices, with_halo(): lax.ppermute(lax.slice_in_dim(block, 0, width, axis=dim), axis, backward)  9.05 us
    dot_general x1, matrix products, local(): lax.dot_general(rotation, lax.all_gather(local_rows, 'vec', axis=0, tiled...  5.65 us
  transfers between devices with their start and end apart: 9, of which 5 were waited for; matrix products, arithmetic and copies ran while one was open for 0% of the time, Pallas kernels for 0%

commit v1 on v0

--- a/solution.py
+++ b/solution.py
@@ -51,7 +51,9 @@
     contract = (((0,), (1,)), ((), ()))
     vec_panel = lax.dot_general(
         rotation,
-        lax.all_gather(local_rows, "vec", axis=0, tiled=True),
+        jnp.concatenate(
+            lax.all_to_all(jnp.stack([local_rows] * lax.axis_size("vec")), "vec", 0, 0), axis=0
+        ),
         contract,
         preferred_element_type=jnp.float32,
     ).astype(jnp.bfloat16)

time: 267 us -> 479 us (1.79)
  waiting for transfers between devices: 168 us -> 376 us
  starting transfers between devices: 26.3 us -> 40.4 us
  between operations: 13.6 us -> 0.25 us
  local copies, waits for them, and re-layouts: 5.19 us -> 10.4 us
    all_to_all x0 -> x1, waiting for transfers between devices: none -> 366 us  [local(): lax.all_to_all(jnp.stack([local_rows] * lax.axis_size('vec')), 'vec', 0, 0)]
    all_gather x1 -> x0, waiting for transfers between devices: 157 us -> none  [local(): lax.all_gather(local_rows, 'vec', axis=0, tiled=True)]
    all_to_all x0 -> x1, starting transfers between devices: none -> 19.7 us  [local(): lax.all_to_all(jnp.stack([local_rows] * lax.axis_size('vec')), 'vec', 0, 0)]
    ppermute x4, starting transfers between devices: 17.3 us -> 11.7 us  [with_halo(): lax.ppermute(lax.slice_in_dim(block, block.shape[dim] - width, None, axis...]
    another operation x0 -> x1, local copies, waits for them, and re-layouts: none -> 5.22 us  [local(): jnp.stack([local_rows] * lax.axis_size('vec'))]
where the time goes in v1:
time: 479 us; the launch traced here: 478 us
  waiting for transfers between devices  376 us (78%)
  starting transfers between devices  40.4 us (8%)
  matrix products  28.3 us (6%)
  blocking collectives  22.1 us (5%)
  local copies, waits for them, and re-layouts  10.4 us (2%)
    all_to_all x1, waiting for transfers between devices, local(): lax.all_to_all(jnp.stack([local_rows] * lax.axis_size('vec')), 'vec', 0, 0)  366 us
    dot_general x4, matrix products, apply_matrix(): jnp.einsum('rjab,krjb->kra', blocks, picked, preferred_element_type=jnp.f...  22.6 us
    all_to_all x1, blocking collectives, local(): lax.all_to_all(filtered, 'vec', split_axis=1, concat_axis=0, tiled=True)  22.1 us
    all_to_all x1, starting transfers between devices, local(): lax.all_to_all(jnp.stack([local_rows] * lax.axis_size('vec')), 'vec', 0, 0)  19.7 us
    ppermute x4, starting transfers between devices, with_halo(): lax.ppermute(lax.slice_in_dim(block, block.shape[dim] - width, None, axis...  11.7 us
    ppermute x4, waiting for transfers between devices, with_halo(): lax.ppermute(lax.slice_in_dim(block, 0, width, axis=dim), axis, backward)  10.7 us
  transfers between devices with their start and end apart: 9, of which 5 were waited for; matrix products, arithmetic and copies ran while one was open for 0% of the time, Pallas kernels for 0%

profile of v1, /device:TPU:1, one launch (start us, length us, event | category | flops | bytes accessed | tf_op | source)
XLA Modules:
  0.0 478.5 jit_solution(16152196805968019871)
XLA Ops:
  0.0 0.0 copy-start
  0.0 5.2 %stack.3 = bf16[64,64,1024]{2,1,0:T(8,128)(2,1)} broadcast(bf16[64,1024]{1,0:T(8,128)(2,1)} %bitcast.133), dimensions={1,2} | broadcast | bytes 8519680 | tf_op jit(solution)/shard_map/stack | solution.py:55
  5.2 0.0 copy-start.1
  5.2 19.7 %all-to-all-start = ((bf16[64,64,1024]{2,1,0:T(8,128)(2,1)}), bf16[64,64,1024]{2,1,0:T(8,128)(2,1)}, u32[]{:S(2)}, u32[]{:S(2)}) async-start(bf16[64,64,1024]{2,1,0:T(8,128)(2,1)} %stack.3), calls=%async_computation | async-start | bytes 16777216 | tf_op jit(solution)/shard_map/all_to_all | solution.py:55
  24.9 0.0 copy-done.1
  24.9 0.1 copy.14
  25.0 0.1 reshape.42
  25.1 365.7 %all-to-all-done = bf16[64,64,1024]{2,1,0:T(8,128)(2,1)} async-done(((bf16[64,64,1024]{2,1,0:T(8,128)(2,1)}), bf16[64,64,1024]{2,1,0:T(8,128)(2,1)}, u32[]{:S(2)}, u32[]{:S(2)}) %all-to-all-start) | async-done | bytes 8388640 | tf_op jit(solution)/shard_map/all_to_all | solution.py:55
  390.8 0.0 copy-done
  390.8 5.7 %convolution_convert_fusion = bf16[16,4096]{1,0:T(8,128)(2,1)S(1)} fusion(bf16[1024,16]{0,1:T(8,128)(2,1)S(1)} %copy-done, bf16[4096,1024]{1,0:T(8,128)(2,1)} %bitcast.1), kind=kOutput, calls=%fused_computation.4 | convolution fusion | flops 134283264 | bytes 8552448 | tf_op jit(solution)/shard_map/dot_general | solution.py:52
  396.4 5.8 %collective-permute-start = (bf16[16,256]{1,0:T(8,128)(2,1)S(1)}, bf16[16,256]{1,0:T(8,128)(2,1)S(1)}, u32[]{:S(2)}, u32[]{:S(2)}) collective-permute-start(bf16[16,256]{1,0:T(8,128)(2,1)S(1)} %get-tuple-element.11), channel_id=1, source_target_pairs={{0,1},{1,2},{2,3},{3,4},{4,5},{5,6},{6,7},{8,9},{9,10},{10,11},{11... | collective-permute-start | bytes 24584 | tf_op jit(solution)/shard_map/ppermute | solution.py:18
  402.3 1.9 collective-permute-start.1
  404.2 0.0 collective-permute-done
  404.2 3.0 collective-permute-done.1
  407.3 0.8 gather_fusion
  408.1 5.7 %convolution_bitcast_fusion.3 = f32[32,2,8,128]{3,2,1,0:T(8,128)S(1)} fusion(bf16[16,32,8,128]{3,0,2,1:T(8,128)(2,1)S(1)} %bitcast.128, bf16[32,8,128,128]{3,2,1,0:T(8,128)(2,1)} %param.6), kind=kOutput, calls=%fused_computation.8 | convolution fusion | flops 134217728 | bytes 9699328 | tf_op jit(solution)/shard_map/rjab,krjb->kra/dot_general | solution.py:30
  413.8 0.1 multiply_convert_fusion
  413.9 1.9 collective-permute-start.2
  415.8 2.4 collective-permute-start.3
  418.2 0.0 collective-permute-done.2
  418.2 2.6 collective-permute-done.3
  420.8 0.8 gather_fusion.1
  421.7 5.7 %convolution_bitcast_fusion.2 = f32[32,2,8,128]{3,2,1,0:T(8,128)S(1)} fusion(bf16[16,32,8,128]{3,0,2,1:T(8,128)(2,1)S(1)} %bitcast.129, bf16[32,8,128,128]{3,2,1,0:T(8,128)(2,1)} %param.6), kind=kOutput, calls=%fused_computation.7 | convolution fusion | flops 134217728 | bytes 9699328 | tf_op jit(solution)/shard_map/rjab,krjb->kra/dot_general | solution.py:30
  427.3 0.1 fusion.8
  427.4 1.9 collective-permute-start.4
  429.4 2.4 collective-permute-start.5
  431.8 0.0 collective-permute-done.4
  431.8 2.6 collective-permute-done.5
  434.4 0.8 gather_fusion.2
  435.2 5.7 %convolution_bitcast_fusion.1 = f32[32,2,8,128]{3,2,1,0:T(8,128)S(1)} fusion(bf16[16,32,8,128]{3,0,2,1:T(8,128)(2,1)S(1)} %bitcast.130, bf16[32,8,128,128]{3,2,1,0:T(8,128)(2,1)} %param.6), kind=kOutput, calls=%fused_computation.6 | convolution fusion | flops 134217728 | bytes 9699328 | tf_op jit(solution)/shard_map/rjab,krjb->kra/dot_general | solution.py:30
  440.9 0.1 fusion.7
  441.0 1.9 collective-permute-start.6
  443.0 2.4 collective-permute-start.7
  445.4 0.0 collective-permute-done.6
  445.4 2.6 collective-permute-done.7
  448.0 0.8 gather_fusion.3
  448.8 5.7 %convolution_bitcast_fusion = f32[32,2,8,128]{3,2,1,0:T(8,128)S(1)} fusion(bf16[16,32,8,128]{3,0,2,1:T(8,128)(2,1)S(1)} %bitcast.127, bf16[32,8,128,128]{3,2,1,0:T(8,128)(2,1)} %param.6), kind=kOutput, calls=%fused_computation.5 | convolution fusion | flops 134217728 | bytes 9699328 | tf_op jit(solution)/shard_map/rjab,krjb->kra/dot_general | solution.py:30
  454.5 0.2 fusion.3
  454.7 0.2 all_to_all.18
  454.9 0.2 copy.72
  455.1 0.2 reshape.84
  455.3 22.1 %all_to_all.24 = bf16[64,2,512]{2,1,0:T(2,128)(2,1)S(1)} all-to-all(bf16[64,2,512]{2,1,0:T(2,128)(2,1)S(1)} %reshape.84), channel_id=1, replica_groups=mesh['vec'=64,'row'=8] {'vec'}, dimensions={0} | all-to-all | bytes 262144 | tf_op jit(solution)/shard_map/all_to_all | solution.py:61
  477.4 0.2 reshape.85
  477.7 0.8 copy.24
  (10 shorter events, 0.1 us)
Async XLA Ops:
  0.0 390.8 %copy-start = (bf16[1024,16]{0,1:T(8,128)(2,1)S(1)}, bf16[1024,16]{0,1:T(8,128)(2,1)}, u32[]{:S(2)}) copy-start(bf16[1024,16]{0,1:T(8,128)(2,1)} %param.5) | copy-start | bytes 98308
  5.2 19.7 %copy-start.1 = (s32[32,8]{0,1:T(8,128)S(1)}, s32[32,8]{0,1:T(8,128)}, u32[]{:S(2)}) copy-start(s32[32,8]{0,1:T(8,128)} %param.7) | copy-start | bytes 3076
  5.2 385.5 %all-to-all-start = ((bf16[64,64,1024]{2,1,0:T(8,128)(2,1)}), bf16[64,64,1024]{2,1,0:T(8,128)(2,1)}, u32[]{:S(2)}, u32[]{:S(2)}) async-start(bf16[64,64,1024]{2,1,0:T(8,128)(2,1)} %stack.3), calls=%async_computation | async-start | bytes 16777216 | tf_op jit(solution)/shard_map/all_to_all | solution.py:55
  396.4 7.8 %collective-permute-start = (bf16[16,256]{1,0:T(8,128)(2,1)S(1)}, bf16[16,256]{1,0:T(8,128)(2,1)S(1)}, u32[]{:S(2)}, u32[]{:S(2)}) collective-permute-start(bf16[16,256]{1,0:T(8,128)(2,1)S(1)} %get-tuple-element.11), channel_id=1, source_target_pairs={{0,1},{1,2},{2,3},{3,4},{4,5},{5,6},{6,7},{8,9},{9,10},{10,11},{11... | collective-permute-start | bytes 24584 | tf_op jit(solution)/shard_map/ppermute | solution.py:18
  402.3 5.0 %collective-permute-start.1 = (bf16[16,256]{1,0:T(8,128)(2,1)S(1)}, bf16[16,256]{1,0:T(8,128)(2,1)S(1)}, u32[]{:S(2)}, u32[]{:S(2)}) collective-permute-start(bf16[16,256]{1,0:T(8,128)(2,1)S(1)} %get-tuple-element.12), channel_id=1, source_target_pairs={{1,0},{2,1},{3,2},{4,3},{5,4},{6,5},{7,6},{9,8},{10,9},{11,10},{12... | collective-permute-start | bytes 24584 | tf_op jit(solution)/shard_map/ppermute | solution.py:21
  413.9 4.3 collective-permute-start.2
  415.8 5.0 %collective-permute-start.3 = (bf16[16,256]{1,0:T(8,128)(2,1)S(1)}, bf16[16,256]{1,0:T(8,128)(2,1)S(1)}, u32[]{:S(2)}, u32[]{:S(2)}) collective-permute-start(bf16[16,256]{1,0:T(8,128)(2,1)S(1)} %get-tuple-element.10), channel_id=1, source_target_pairs={{1,0},{2,1},{3,2},{4,3},{5,4},{6,5},{7,6},{9,8},{10,9},{11,10},{12... | collective-permute-start | bytes 24584 | tf_op jit(solution)/shard_map/ppermute | solution.py:21
  427.4 4.3 collective-permute-start.4
  429.4 5.0 %collective-permute-start.5 = (bf16[16,256]{1,0:T(8,128)(2,1)S(1)}, bf16[16,256]{1,0:T(8,128)(2,1)S(1)}, u32[]{:S(2)}, u32[]{:S(2)}) collective-permute-start(bf16[16,256]{1,0:T(8,128)(2,1)S(1)} %get-tuple-element.8), channel_id=1, source_target_pairs={{1,0},{2,1},{3,2},{4,3},{5,4},{6,5},{7,6},{9,8},{10,9},{11,10},{12... | collective-permute-start | bytes 24584 | tf_op jit(solution)/shard_map/ppermute | solution.py:21
  441.0 4.3 collective-permute-start.6
  443.0 5.0 %collective-permute-start.7 = (bf16[16,256]{1,0:T(8,128)(2,1)S(1)}, bf16[16,256]{1,0:T(8,128)(2,1)S(1)}, u32[]{:S(2)}, u32[]{:S(2)}) collective-permute-start(bf16[16,256]{1,0:T(8,128)(2,1)S(1)} %get-tuple-element.6), channel_id=1, source_target_pairs={{1,0},{2,1},{3,2},{4,3},{5,4},{6,5},{7,6},{9,8},{10,9},{11,10},{12... | collective-permute-start | bytes 24584 | tf_op jit(solution)/shard_map/ppermute | solution.py:21
